TPU v7x, 32 devices: a whole 2x2x4 slice. The times are simulated.
32 devices in a mesh: pw: 2 (over y), tile: 16 (over z, x, core).
Axes of the slice: x: 2, y: 2, z: 4, core: 2. Of those that a mesh axis runs over, the one named last changes fastest.
Arguments:
- mask_tiles: float32 [4, 256, 4096], P(None, None, 'tile'), may hold values from 0 to 1
- target_print: float32 [4, 256, 4096], P(None, None, 'tile'), may hold values from 0 to 1
- geometry_flags: int32 [4, 16], P(None, 'tile'), may hold values from 0 to 1, as said below
- kernel_taps: float32 [2, 12, 4, 129], P('pw'), may hold values from -0.5 to 0.5
- dose_factor: float32 [2], P('pw'), may hold values from 0.7 to 1.4
Outputs:
- mask_gradient: float32 [4, 256, 4096], P(None, 'pw', 'tile')
Inputs may be any that keep to these rules, and one draw needn't show every extreme that they name: `geometry_flags`: every tile column has at most 1 tiles with geometry, and some column has exactly 1.
All inputs are finite; a program needn't handle non-finite values.
Results may differ from a plain program's by a relative error of at most 0.0089.
Values may be sent and summed in bfloat16 or wider, within the bound.
A program may use at most 128 MiB of HBM per device.

v0:
```python
import jax
import jax.numpy as jnp
from jax import lax
from jax.sharding import PartitionSpec as P

TILE = 256
AMBIT = 64
KERNELS = 12
TILE_ROWS = 4
ACTIVE_MOST = 1
TAPS = 129
EXTENT = 384


STEEP = 4.0
THRESHOLD = 1.3
LOSS_WEIGHT = 4.0


def padded_2(shard, sides, width):
    for axis, dim in sides:
        count, length = (lax.axis_size(axis), shard.shape[dim])
        up = [(i, (i + 1) % count) for i in range(count - 1)]
        down = [(j, i) for i, j in up]
        last = lax.slice_in_dim(shard, length - width, length, axis=dim)
        first = lax.slice_in_dim(shard, 0, width, axis=dim)
        before = lax.ppermute(last, axis, up)
        after = lax.ppermute(first, axis, down)
        shard = jnp.concatenate([before, shard, after], axis=dim)
    return shard


def skew_band(taps_low):
    lead = taps_low.shape[:-1]
    padded = jnp.pad(taps_low, [(0, 0)] * len(lead) + [(0, EXTENT + 1 - TAPS)])
    repeated = jnp.tile(padded, (1,) * len(lead) + (TILE,))
    return repeated[..., : TILE * EXTENT].reshape(lead + (TILE, EXTENT))


def build_tables(taps_one):
    bands = skew_band(taps_one.astype(jnp.bfloat16))
    row_real = bands[:, 0]
    row_imag = bands[:, 1]
    col_real = bands[:, 2]
    col_imag = bands[:, 3]
    fwd_rows = bands[:, 0:2]
    fwd_cols = jnp.concatenate(
        [
            jnp.concatenate([col_real, -col_imag], axis=2),
            jnp.concatenate([col_imag, col_real], axis=2),
        ],
        axis=1,
    )
    adj_cols = jnp.concatenate(
        [
            jnp.concatenate([col_real, col_imag], axis=2),
            jnp.concatenate([col_imag, -col_real], axis=2),
        ],
        axis=1,
    )
    adj_rows = jnp.stack([row_real, -row_imag], axis=2)
    return (fwd_rows, fwd_cols, adj_cols, adj_rows)


def tile_gradient(window, goal_tile, live_weight, dose_value, tables):
    fwd_rows, fwd_cols, adj_cols, adj_rows = tables
    partial_field = jnp.einsum(
        "kcte,ef->ktcf", fwd_rows, window, preferred_element_type=jnp.float32
    )
    partial_field = partial_field.reshape(KERNELS, TILE, 2 * EXTENT).astype(jnp.bfloat16)
    field_all = jnp.einsum(
        "ktf,ksf->kts", partial_field, fwd_cols, preferred_element_type=jnp.float32
    )
    real_field = field_all[:, :, :TILE]
    imag_field = field_all[:, :, TILE:]
    intensity = (
        dose_value / KERNELS * jnp.sum(real_field * real_field + imag_field * imag_field, axis=0)
    )
    resist = jax.nn.sigmoid(STEEP * (intensity - THRESHOLD))
    sensitivity = (
        live_weight
        * LOSS_WEIGHT
        * 2.0
        * (resist - goal_tile)
        * resist
        * (1.0 - resist)
        * STEEP
        * dose_value
        / KERNELS
    )
    weighted = (field_all * jnp.concatenate([sensitivity, sensitivity], axis=1)[None]).astype(
        jnp.bfloat16
    )
    adjoint = jnp.einsum(
        "kts,ksf->ktf", weighted, adj_cols, preferred_element_type=jnp.float32
    ).astype(jnp.bfloat16)
    adjoint = adjoint.reshape(KERNELS, TILE, 2, EXTENT)
    return 2.0 * jnp.einsum("ktce,ktcf->ef", adj_rows, adjoint, preferred_element_type=jnp.float32)


def fold_rims(rimmed):
    inner = rimmed[..., 2 * AMBIT : 2 * AMBIT + TILE]
    inner = inner.at[..., :AMBIT].add(rimmed[..., :AMBIT])
    return inner.at[..., TILE - AMBIT :].add(rimmed[..., AMBIT + EXTENT :])


def on_device(mask_tiles, target_print, geometry_flags, kernel_taps, dose_factor):
    band_rows = TILE_ROWS * TILE
    mask_band = mask_tiles.astype(jnp.bfloat16).reshape(band_rows, TILE)
    widened = padded_2(mask_band, (("tile", 1),), AMBIT)
    padded = jnp.pad(widened, ((AMBIT, AMBIT), (0, 0)))
    goal_band = target_print.reshape(band_rows, TILE)
    present = geometry_flags[:, 0]
    position = jnp.cumsum(present) - 1
    live_count = jnp.sum(present)
    target_slot = jnp.where(present > 0, position, ACTIVE_MOST)
    slot_tile = (
        jnp.zeros((ACTIVE_MOST,), jnp.int32)
        .at[target_slot]
        .set(jnp.arange(TILE_ROWS, dtype=jnp.int32), mode="drop")
    )
    live_slots = (jnp.arange(ACTIVE_MOST, dtype=jnp.int32) < live_count).astype(jnp.float32)
    tables = build_tables(kernel_taps[0])
    dose_value = dose_factor[0]

    def add_tile(slot_number, buffer):
        row_start = slot_tile[slot_number] * TILE
        col_start = jnp.int32(0)
        window = lax.dynamic_slice(padded, (row_start, col_start), (EXTENT, EXTENT))
        goal_tile = lax.dynamic_slice(goal_band, (row_start, col_start), (TILE, TILE))
        tile_grad = tile_gradient(window, goal_tile, live_slots[slot_number], dose_value, tables)
        current = lax.dynamic_slice(buffer, (row_start, col_start), (EXTENT, EXTENT))
        return lax.dynamic_update_slice(buffer, current + tile_grad, (row_start, col_start))

    buffer = lax.fori_loop(
        0, ACTIVE_MOST, add_tile, jnp.zeros((band_rows + 2 * AMBIT, EXTENT), jnp.float32)
    )
    band_grad = buffer[AMBIT : AMBIT + band_rows]
    rimmed = padded_2(band_grad, (("tile", 1),), AMBIT)
    owned = fold_rims(rimmed).reshape(TILE_ROWS, TILE, TILE)
    return lax.psum_scatter(owned, "pw", scatter_dimension=1, tiled=True)


def solution(mesh):
    return jax.shard_map(
        on_device,
        mesh=mesh,
        in_specs=(
            P(None, None, "tile"),
            P(None, None, "tile"),
            P(None, "tile"),
            P("pw", None, None, None),
            P("pw"),
        ),
        out_specs=P(None, "pw", "tile"),
        check_vma=False,
    )
```

profile of v0, /device:TPU:1, one launch (start us, length us, event | category | flops | bytes accessed | tf_op | source)
XLA Modules:
  0.0 150.9 jit_solution(17972565010978082314)
XLA Ops:
  6.5 0.0 reduce-scatter.2.cloned.1.call-start
  6.5 1.3 convert_element_type.34
  7.8 0.2 copy.21
  8.1 4.5 %collective-permute-start = (bf16[1024,64]{0,1:T(8,128)(2,1)S(1)}, bf16[1024,64]{0,1:T(8,128)(2,1)S(1)}, u32[]{:S(2)}, u32[]{:S(2)}) collective-permute-start(bf16[1024,64]{0,1:T(8,128)(2,1)S(1)} %get-tuple-element.74), channel_id=1, source_target_pairs={{0,1},{1,2},{2,3},{3,4},{4,5},{5,6},{6,7},{7,8},{8,9},{9,10},{10,1... | collective-permute-start | bytes 393224 | tf_op jit(solution)/shard_map/ppermute | solution.py:27
  12.6 1.9 %collective-permute-start.1 = (bf16[1024,64]{0,1:T(8,128)(2,1)S(1)}, bf16[1024,64]{0,1:T(8,128)(2,1)S(1)}, u32[]{:S(2)}, u32[]{:S(2)}) collective-permute-start(bf16[1024,64]{0,1:T(8,128)(2,1)S(1)} %get-tuple-element.73), channel_id=1, source_target_pairs={{1,0},{2,1},{3,2},{4,3},{5,4},{6,5},{7,6},{8,7},{9,8},{10,9},{11,1... | collective-permute-start | bytes 393224 | tf_op jit(solution)/shard_map/ppermute | solution.py:28
  14.5 0.8 convert_bitcast_fusion
  15.3 5.5 %tile.4 = bf16[12,4,256,385]{3,2,1,0:T(8,128)(2,1)} broadcast(bf16[12,4,385]{2,1,0:T(4,128)(2,1)S(1)} %pad.12), dimensions={0,1,3} | broadcast | bytes 9498720 | tf_op jit(solution)/shard_map/tile | solution.py:36
  20.8 21.0 %tile.10 = bf16[12,4,98560]{2,1,0:T(4,128)(2,1)} reshape(bf16[12,4,256,385]{3,2,1,0:T(8,128)(2,1)} %tile.4) | data formatting | bytes 18923520 | tf_op jit(solution)/shard_map/tile | solution.py:36
  41.8 8.5 %slice.101 = bf16[12,4,98304]{2,1,0:T(4,128)(2,1)} slice(bf16[12,4,98560]{2,1,0:T(4,128)(2,1)} %tile.10), slice={[0:12], [0:4], [0:98304]} | slice | bytes 18874368 | tf_op jit(solution)/shard_map/slice | solution.py:37
  50.3 13.0 %reshape.109 = bf16[12,4,256,384]{3,2,1,0:T(8,128)(2,1)} reshape(bf16[12,4,98304]{2,1,0:T(4,128)(2,1)} %slice.101) | data formatting | bytes 18874368 | tf_op jit(solution)/shard_map/reshape | solution.py:37
  63.3 0.0 copy-start
  63.3 6.6 %slice_bitcast_fusion.1 = (bf16[12,256,384]{2,1,0:T(8,128)(2,1)}, bf16[12,256,384]{2,1,0:T(8,128)(2,1)}, bf16[12,256,1,384]{3,1,0,2:T(8,128)(2,1)S(1)}, bf16[12,256,1,384]{3,1,0,2:T(8,128)(2,1)}) fusion(bf16[12,4,256,384]{3,2,1,0:T(8,128)(2,1)} %reshape.109), kind=kLoop, calls=%fused_computation.32 | loop fusion | flops 1179648 | bytes 18874368 | tf_op jit(solution)/shard_map/squeeze | solution.py:45
  69.9 2.4 %copy-done = bf16[12,4,256,384]{3,2,1,0:T(8,128)(2,1)S(1)} copy-done((bf16[12,4,256,384]{3,2,1,0:T(8,128)(2,1)S(1)}, bf16[12,4,256,384]{3,2,1,0:T(8,128)(2,1)}, u32[]{:S(2)}) %copy-start) | copy-done | bytes 9437208
  72.3 0.0 copy-start.1
  72.3 2.6 %fusion.72 = (bf16[12,256,384]{2,1,0:T(8,128)(2,1)}, bf16[12,256,384]{2,1,0:T(8,128)(2,1)}) fusion(bf16[12,4,256,384]{3,2,1,0:T(8,128)(2,1)S(1)} %copy-done), kind=kLoop, calls=%fused_computation.75 | loop fusion | flops 2359296 | bytes 9437184 | tf_op jit(solution)/shard_map/neg | solution.py:49
  74.9 0.0 copy-done.1
  74.9 0.2 reduce-window.4
  75.1 0.6 reduce_sum.19
  75.8 1.6 %scatter_fusion = s32[1]{0:T(128)} fusion(s32[1]{0:T(128)} %copy.41, s32[4]{0:T(128)S(1)} %fusion.63, s32[4]{0:T(128)S(1)} %iota.7), kind=kCustom, calls=%fused_computation | custom fusion | bytes 64 | tf_op jit(solution)/shard_map/scatter | solution.py:120
  79.2 0.0 collective-permute-done
  79.3 0.0 collective-permute-done.1
  79.3 7.7 %fusion.24 = bf16[384,12,2,256]{3,0,2,1:T(8,128)(2,1)} fusion(bf16[12,4,256,384]{3,2,1,0:T(8,128)(2,1)} %reshape.109, s32[]{:T(128)S(6)} %select_n.24, bf16[1024,64]{0,1:T(8,128)(2,1)S(1)} %collective-permute-done, bf16[1024,256]{0,1:T(8,128)(2,1)S(1)} %copy.21, bf16[1024,64]{0,1:T(8,128)(2,1)S(1)} %collective-permute-done.1), kind=kOutput, calls=%fused_computation.28 | convolution fusion | flops 1816215552 | bytes 10224640 | tf_op jit(solution)/shard_map/while/body/eval_jaxpr/kcte,ef->ktcf/dot_general | solution.py:67
  86.9 7.1 %fusion.1 = f32[12,256,512]{2,1,0:T(8,128)S(1)} fusion(bf16[12,256,768]{1,2,0:T(8,128)(2,1)} %bitcast.59, bf16[12,256,384]{2,1,0:T(8,128)(2,1)} %get-tuple-element.68, bf16[12,256,384]{2,1,0:T(8,128)(2,1)} %get-tuple-element.67, bf16[12,256,384]{2,1,0:T(8,128)(2,1)} %get-tuple-element.65), kind=kOutput, calls=%fused_computation.6 | convolution fusion | flops 2453667840 | bytes 18087936 | tf_op jit(solution)/shard_map/while/body/eval_jaxpr/ktf,ksf->kts/dot_general | solution.py:71
  94.0 0.4 fusion.19
  94.4 1.1 multiply_multiply_fusion
  95.6 7.7 %fusion.21 = bf16[12,256,768]{2,1,0:T(8,128)(2,1)} fusion(bf16[12,256,384]{2,1,0:T(8,128)(2,1)} %get-tuple-element.68, bf16[12,256,384]{2,1,0:T(8,128)(2,1)} %get-tuple-element.67, bf16[12,256,384]{2,1,0:T(8,128)(2,1)} %get-tuple-element.66, f32[12,256,512]{2,1,0:T(8,128)S(1)} %fusion.1, f32[256,512]{1,0:T(8,128)S(1)} %pad_maximum_fusion.6), kind=kOutput, calls=%fused_computation.27 | convolution fusion | flops 2459172864 | bytes 18612224 | tf_op jit(solution)/shard_map/while/body/eval_jaxpr/kts,ksf->ktf/dot_general | solution.py:94
  103.2 0.1 broadcast_in_dim.8
  103.4 5.7 %fusion.38 = f32[1152,384]{0,1:T(8,128)S(1)} fusion(f32[1152,384]{0,1:T(8,128)S(1)} %broadcast_in_dim.8, s32[]{:T(128)S(6)} %select_n.24, bf16[12,256,1,384]{3,1,0,2:T(8,128)(2,1)S(1)} %get-tuple-element.69, bf16[12,256,1,384]{3,1,0,2:T(8,128)(2,1)} %get-tuple-element.70, bf16[12,32,2,8,384]{4,3,2,1,0:T(8,128)(2,1)} %bitcast.58), kind=kOutput, calls=%fused_computation.36 | convolution fusion | flops 1814446080 | bytes 10027012 | tf_op jit(solution)/shard_map/while/body/eval_jaxpr/ktce,ktcf->ef/dot_general | solution.py:98
  109.1 0.2 fusion.73
  109.3 3.6 %collective-permute-start.2 = (f32[1024,64]{0,1:T(8,128)S(1)}, f32[1024,64]{0,1:T(8,128)S(1)}, u32[]{:S(2)}, u32[]{:S(2)}) collective-permute-start(f32[1024,64]{0,1:T(8,128)S(1)} %get-tuple-element.72), channel_id=1, source_target_pairs={{0,1},{1,2},{2,3},{3,4},{4,5},{5,6},{6,7},{7,8},{8,9},{9,10},{10,1... | collective-permute-start | bytes 786440 | tf_op jit(solution)/shard_map/ppermute | solution.py:27
  112.9 1.9 %collective-permute-start.3 = (f32[1024,64]{0,1:T(8,128)S(1)}, f32[1024,64]{0,1:T(8,128)S(1)}, u32[]{:S(2)}, u32[]{:S(2)}) collective-permute-start(f32[1024,64]{0,1:T(8,128)S(1)} %get-tuple-element.71), channel_id=1, source_target_pairs={{1,0},{2,1},{3,2},{4,3},{5,4},{6,5},{7,6},{8,7},{9,8},{10,9},{11,1... | collective-permute-start | bytes 786440 | tf_op jit(solution)/shard_map/ppermute | solution.py:28
  114.9 0.6 compare_reduce_fusion
  115.5 0.3 slice.109
  115.9 0.4 collective-permute-done.2
  116.2 0.8 fusion.59
  117.0 3.6 %collective-permute-done.3 = f32[1024,64]{0,1:T(8,128)S(1)} collective-permute-done((f32[1024,64]{0,1:T(8,128)S(1)}, f32[1024,64]{0,1:T(8,128)S(1)}, u32[]{:S(2)}, u32[]{:S(2)}) %collective-permute-start.3) | collective-permute-done | bytes 262176 | tf_op jit(solution)/shard_map/ppermute | solution.py:28
  120.6 0.1 fusion.60
  120.7 1.3 copy.17
  122.0 0.0 reduce-scatter.2.cloned.1.call-update
  122.1 22.0 %reduce-scatter.2.cloned.1.call-done = f32[4,128,256]{2,1,0:T(8,128)} async-done(((f32[4,256,256]{2,1,0:T(8,128)}), f32[4,128,256]{2,1,0:T(8,128)}) %reduce-scatter.2.cloned.1.call-update) | async-done | bytes 524304 | tf_op jit(solution)/shard_map/reduce_scatter | solution.py:141
  (5 shorter events, 0.1 us)
Async XLA Ops:
  6.5 137.5 %reduce-scatter.2.cloned.1.call-start = ((), (), s32[]{:S(2)}) async-start(), calls=%async_computation.1 | async-start | bytes 1572864 | tf_op jit(solution)/shard_map/reduce_scatter | solution.py:141
  8.1 71.2 %collective-permute-start = (bf16[1024,64]{0,1:T(8,128)(2,1)S(1)}, bf16[1024,64]{0,1:T(8,128)(2,1)S(1)}, u32[]{:S(2)}, u32[]{:S(2)}) collective-permute-start(bf16[1024,64]{0,1:T(8,128)(2,1)S(1)} %get-tuple-element.74), channel_id=1, source_target_pairs={{0,1},{1,2},{2,3},{3,4},{4,5},{5,6},{6,7},{7,8},{8,9},{9,10},{10,1... | collective-permute-start | bytes 393224 | tf_op jit(solution)/shard_map/ppermute | solution.py:27
  12.6 66.7 %collective-permute-start.1 = (bf16[1024,64]{0,1:T(8,128)(2,1)S(1)}, bf16[1024,64]{0,1:T(8,128)(2,1)S(1)}, u32[]{:S(2)}, u32[]{:S(2)}) collective-permute-start(bf16[1024,64]{0,1:T(8,128)(2,1)S(1)} %get-tuple-element.73), channel_id=1, source_target_pairs={{1,0},{2,1},{3,2},{4,3},{5,4},{6,5},{7,6},{8,7},{9,8},{10,9},{11,1... | collective-permute-start | bytes 393224 | tf_op jit(solution)/shard_map/ppermute | solution.py:28
  63.3 9.0 %copy-start = (bf16[12,4,256,384]{3,2,1,0:T(8,128)(2,1)S(1)}, bf16[12,4,256,384]{3,2,1,0:T(8,128)(2,1)}, u32[]{:S(2)}) copy-start(bf16[12,4,256,384]{3,2,1,0:T(8,128)(2,1)} %reshape.109) | copy-start | bytes 28311556
  72.3 2.6 %copy-start.1 = (s32[4,1]{0,1:T(1,128)S(1)}, s32[4,1]{0,1:T(1,128)}, u32[]{:S(2)}) copy-start(s32[4,1]{0,1:T(1,128)} %param.11) | copy-start | bytes 52
  109.3 6.9 %collective-permute-start.2 = (f32[1024,64]{0,1:T(8,128)S(1)}, f32[1024,64]{0,1:T(8,128)S(1)}, u32[]{:S(2)}, u32[]{:S(2)}) collective-permute-start(f32[1024,64]{0,1:T(8,128)S(1)} %get-tuple-element.72), channel_id=1, source_target_pairs={{0,1},{1,2},{2,3},{3,4},{4,5},{5,6},{6,7},{7,8},{8,9},{9,10},{10,1... | collective-permute-start | bytes 786440 | tf_op jit(solution)/shard_map/ppermute | solution.py:27
  112.9 7.7 %collective-permute-start.3 = (f32[1024,64]{0,1:T(8,128)S(1)}, f32[1024,64]{0,1:T(8,128)S(1)}, u32[]{:S(2)}, u32[]{:S(2)}) collective-permute-start(f32[1024,64]{0,1:T(8,128)S(1)} %get-tuple-element.71), channel_id=1, source_target_pairs={{1,0},{2,1},{3,2},{4,3},{5,4},{6,5},{7,6},{8,7},{9,8},{10,9},{11,1... | collective-permute-start | bytes 786440 | tf_op jit(solution)/shard_map/ppermute | solution.py:28
Sparse Core Ops, SparseCore 0:
  122.2 21.8 reduce-scatter.1
where the time goes:
time: 153 us; the launch traced here: 151 us
  local copies, waits for them, and re-layouts  54.3 us (35%)
  matrix products  28.1 us (18%)
  waiting for transfers between devices  26 us (17%)
  between operations  15.4 us (10%)
  other arithmetic  15.1 us (10%)
  starting transfers between devices  12 us (8%)
    another operation x2, local copies, waits for them, and re-layouts, skew_band(): repeated = jnp.tile(padded, (1,) * len(lead) + (TILE,))  26.5 us
    reduce_scatter x1, waiting for transfers between devices, on_device(): return lax.psum_scatter(owned, 'pw', scatter_dimension=1, tiled=True)  22 us
    reshape x1, local copies, waits for them, and re-layouts, skew_band(): return repeated[..., :TILE * EXTENT].reshape(lead + (TILE, EXTENT))  13 us
    slice x1, local copies, waits for them, and re-layouts, skew_band(): return repeated[..., :TILE * EXTENT].reshape(lead + (TILE, EXTENT))  8.46 us
    ppermute x2, starting transfers between devices, padded_2(): before = lax.ppermute(last, axis, up)  8.14 us
    dot_general x1, matrix products, tile_gradient(): jnp.einsum('kts,ksf->ktf', weighted, adj_cols, preferred_element_type=jnp...  7.66 us
    dot_general x1, matrix products, tile_gradient(): jnp.einsum('kcte,ef->ktcf', fwd_rows, window, preferred_element_type=jnp....  7.65 us
    dot_general x1, matrix products, tile_gradient(): jnp.einsum('ktf,ksf->kts', partial_field, fwd_cols, preferred_element_typ...  7.08 us
  transfers between devices with their start and end apart: 5, of which 3 were waited for; matrix products, arithmetic and copies ran while one was open for 41% of the time, Pallas kernels for 0%

commit v1 on v0

v1 whole, which is shorter than its diff:
```python
import jax
import jax.numpy as jnp
from jax import lax
from jax.experimental import pallas as pl
from jax.experimental.pallas import tpu as pltpu
from jax.sharding import PartitionSpec as P

STEEP = 4.0
THRESHOLD = 1.3
LOSS_WEIGHT = 4.0
LANES = 128
F32 = jnp.float32
BF16 = jnp.bfloat16


def low_lanes(rows, half):
    return lax.broadcasted_iota(jnp.int32, (rows, LANES), 1) < half


def gradient_kernel(
    sizes, mask_hbm, goal_hbm, flags, taps, dose, halos, center, rims,
    mask_f32, goal_f32, row_bands, row_bands_t, col_a, col_b,
    fields_in, fields, intensity, adjoint, local_sem,
):
    pw_count, tile_rows, tile, kernels, ambit = sizes
    height = tile_rows * tile
    extent = tile + 2 * ambit
    own_rows = tile // pw_count
    edge_rows = min(own_rows, ambit)
    pack_rows = own_rows + edge_rows

    mask_copy = pltpu.make_async_copy(mask_hbm, mask_f32.at[ambit:ambit + height], local_sem.at[0])
    mask_copy.start()
    zero_rows = jnp.zeros((ambit, tile), F32)
    mask_f32[0:ambit, :] = zero_rows
    mask_f32[ambit + height:, :] = zero_rows
    live_row = sum(g * flags[g] for g in range(tile_rows))
    live = sum(flags[g] for g in range(tile_rows)).astype(F32)
    window = pl.ds(pl.multiple_of(live_row * tile, tile), extent)
    goal_copy = pltpu.make_async_copy(goal_hbm.at[live_row], goal_f32, local_sem.at[1])
    goal_copy.start()

    def band(k, which):
        row = jnp.broadcast_to(taps[k, which:which + 1, :], (LANES, 2 * LANES))
        return pltpu.roll(row, 0, 1, stride=1, stride_axis=0)

    def build(k, carry):
        row_real, row_imag = band(k, 0).astype(BF16), band(k, 1).astype(BF16)
        col_real, col_imag = band(k, 2), band(k, 3)
        row_bands[k, 0:LANES, :] = row_real
        row_bands[k, LANES:, :] = row_imag
        row_bands_t[k, :, 0:LANES] = row_real.T
        row_bands_t[k, :, LANES:] = row_imag.T
        col_a[k, 0:LANES, :] = col_real.astype(BF16)
        col_a[k, LANES:, :] = col_imag.astype(BF16)
        col_b[k, 0:LANES, :] = (-col_imag).astype(BF16)
        col_b[k, LANES:, :] = col_real.astype(BF16)
        return carry

    lax.fori_loop(0, kernels, build, 0)

    mask_copy.wait()
    low = low_lanes(extent, ambit)
    turned_a = pltpu.roll(mask_f32[window, 0:LANES], ambit, 1)
    turned_b = pltpu.roll(mask_f32[window, LANES:], ambit, 1)
    rim = jnp.where(low, turned_b, turned_a)
    halo = halos[window, :].astype(F32)

    def row_stage(block, at):
        both = jnp.concatenate([block[0:2 * LANES], block[LANES:3 * LANES]], axis=1)

        def one(k):
            z = jnp.dot(row_bands[k], both, preferred_element_type=F32).astype(BF16)
            for part in range(2):
                for i in range(2):
                    fields_in[k, part, i * LANES:(i + 1) * LANES, at * LANES:(at + 1) * LANES] = (
                        z[part * LANES:(part + 1) * LANES, i * LANES:(i + 1) * LANES])

        for k in range(kernels):
            one(k)

    row_stage(jnp.where(low, turned_a, turned_b).astype(BF16), 1)
    row_stage(jnp.where(low, halo, rim).astype(BF16), 0)
    row_stage(jnp.where(low, rim, halo).astype(BF16), 2)

    contract_last = (((1,), (1,)), ((), ()))
    intensity[...] = jnp.zeros_like(intensity)

    def column(k, carry):
        total = None
        for part, table in ((0, col_a), (1, col_b)):
            lhs = jnp.concatenate(
                [fields_in[k, part, :, 0:2 * LANES], fields_in[k, part, :, LANES:3 * LANES]], axis=0)
            term = lax.dot_general(lhs, table[k], contract_last, preferred_element_type=F32)
            total = term if total is None else total + term
        fields[k] = total
        real, imag = total[:, :LANES], total[:, LANES:]
        intensity[...] += real * real + imag * imag
        return carry

    lax.fori_loop(0, kernels, column, 0)

    goal_copy.wait()
    dose_value = dose[0]
    goal = goal_f32[...]
    for j in range(2):
        rows = slice(j * tile, (j + 1) * tile)
        resist = jax.nn.sigmoid(STEEP * (dose_value / kernels * intensity[rows, :] - THRESHOLD))
        wanted = goal[:, j * LANES:(j + 1) * LANES]
        factor = live * LOSS_WEIGHT * 2.0 * STEEP * dose_value / kernels
        intensity[rows, :] = factor * (resist - wanted) * resist * (1.0 - resist)

    def adjoint_stage(k, carry):
        scale = intensity[...]
        weighted = (fields[k] * jnp.concatenate([scale, scale], axis=1)).astype(BF16)
        for part, table in ((0, col_a), (1, col_b)):
            wide = jnp.dot(weighted, table[k], preferred_element_type=F32)
            blocks = (wide[:tile, :LANES], wide[:tile, LANES:] + wide[tile:, :LANES], wide[tile:, LANES:])
            for b, block in enumerate(blocks):
                block = block.astype(BF16)
                for i in range(2):
                    adjoint[b, k, part * LANES:(part + 1) * LANES, i * LANES:(i + 1) * LANES] = (
                        block[i * LANES:(i + 1) * LANES])
        return carry

    lax.fori_loop(0, kernels, adjoint_stage, 0)

    turned = []
    for b in range(3):
        total = jnp.zeros((2 * LANES, 2 * LANES), F32)
        for k in range(kernels):
            total += jnp.dot(row_bands_t[k], adjoint[b, k], preferred_element_type=F32)
        total = 2.0 * total
        rows = jnp.concatenate(
            [total[:LANES, :LANES], total[LANES:, :LANES] + total[:LANES, LANES:], total[LANES:, LANES:]], axis=0)
        turned.append(pltpu.roll(rows, ambit, 1))
    blocks = (jnp.where(low, turned[0], turned[1]), jnp.where(low, turned[1], turned[2]),
              jnp.where(low, turned[2], turned[0]))
    flag_rows = jnp.concatenate(
        [jnp.full((1, LANES), flags[g].astype(F32)) for g in range(tile_rows)]
        + [jnp.zeros((16 - tile_rows, LANES), F32)], axis=0)
    for q in range(pw_count):
        first = ambit + q * own_rows
        if q * own_rows < ambit:
            edge = ambit + tile + q * own_rows
        else:
            edge = max(q * own_rows - (tile - ambit), 0)
        for b, block in enumerate(blocks):
            main = block[first:first + own_rows].astype(BF16)
            side = block[edge:edge + edge_rows].astype(BF16)
            if b < 2:
                center[q, 0:own_rows, b * LANES:(b + 1) * LANES] = main
                center[q, own_rows:, b * LANES:(b + 1) * LANES] = side
            else:
                rims[q, 0:own_rows, :] = main
                rims[q, own_rows:pack_rows, :] = side
                rims[q, pack_rows:, :] = flag_rows.astype(BF16)


def gather_kernel(sizes, flags, place, own_center, *refs):
    pw_count, tile_rows, tile, ambit = sizes
    centers, lefts, rights = refs[:pw_count - 1], refs[pw_count - 1:2 * pw_count - 1], refs[2 * pw_count - 1:-1]
    out_ref = refs[-1]
    own_rows = tile // pw_count
    edge_rows = min(own_rows, ambit)
    pack_rows = own_rows + edge_rows
    p = place[0]
    total = own_center[p].astype(F32)
    for ref in centers:
        total += ref[...].astype(F32)
    left, right = lefts[0][...].astype(F32), rights[0][...].astype(F32)
    left_sum = sum(ref[0:pack_rows, :].astype(F32) for ref in lefts)
    right_sum = sum(ref[0:pack_rows, :].astype(F32) for ref in rights)
    pack_low = low_lanes(pack_rows, ambit)
    left_sum = jnp.where(pack_low, left_sum, 0.0)
    right_sum = jnp.where(pack_low, 0.0, right_sum)
    is_low = jnp.where(p * own_rows < ambit, 1.0, 0.0).astype(F32)
    is_high = jnp.where((p + 1) * own_rows > tile - ambit, 1.0, 0.0).astype(F32)
    halves = ((total[:, :LANES], left_sum, left), (total[:, LANES:], right_sum, right))

    def flag_of(kind, g):
        if g < 0 or g >= tile_rows:
            return None
        if kind is None:
            return flags[g].astype(F32)
        return kind[pack_rows + g:pack_rows + g + 1, :]

    for b, (own, rim, rim_flags) in enumerate(halves):
        lanes = slice(b * LANES, (b + 1) * LANES)
        for g in range(tile_rows):
            out_ref[g, :, lanes] = (
                flag_of(None, g) * own[:own_rows] + flag_of(rim_flags, g) * rim[:own_rows])
            for at, switch, source in ((0, is_low, g - 1), (own_rows - edge_rows, is_high, g + 1)):
                if 0 <= source < tile_rows:
                    out_ref[g, at:at + edge_rows, lanes] += switch * (
                        flag_of(None, source) * own[own_rows:] + flag_of(rim_flags, source) * rim[own_rows:])


def solution(mesh):
    pw_count, tile_count = mesh.shape["pw"], mesh.shape["tile"]

    def on_device(mask_tiles, target_print, geometry_flags, kernel_taps, dose_factor):
        tile_rows, tile, _ = mask_tiles.shape
        kernels, kinds, tap_count = kernel_taps.shape[1:]
        ambit = (tap_count - 1) // 2
        height, extent = tile_rows * tile, tile + 2 * ambit
        own_rows = tile // pw_count
        pack_rows = own_rows + min(own_rows, ambit)
        wide = 2 * LANES
        vmem = pl.BlockSpec(memory_space=pltpu.VMEM)
        smem = pl.BlockSpec(memory_space=pltpu.SMEM)
        anywhere = pl.BlockSpec(memory_space=pl.ANY)
        p = lax.axis_index("pw")
        taps = jnp.pad(kernel_taps[0], ((0, 0), (0, 8 - kinds), (0, wide - tap_count)))
        flags = geometry_flags.reshape(tile_rows)
        mask = mask_tiles.reshape(height, tile)
        right_way = [(i, i + 1) for i in range(tile_count - 1)]
        left_way = [(j, i) for i, j in right_way]
        before = lax.ppermute(mask[:, tile - ambit:].astype(BF16), "tile", right_way)
        after = lax.ppermute(mask[:, :ambit].astype(BF16), "tile", left_way)
        halos = jnp.pad(jnp.concatenate([before, after], axis=1), ((ambit, ambit), (0, 0)))

        def gradient(*refs):
            gradient_kernel((pw_count, tile_rows, tile, kernels, ambit), *refs)

        def gather(*refs):
            gather_kernel((pw_count, tile_rows, tile, ambit), *refs)

        center, rims = pl.pallas_call(
            gradient,
            out_shape=(
                jax.ShapeDtypeStruct((pw_count, pack_rows, tile), BF16),
                jax.ShapeDtypeStruct((pw_count, pack_rows + 16, LANES), BF16),
            ),
            in_specs=[anywhere, anywhere, smem, vmem, smem, vmem],
            out_specs=(vmem, vmem),
            scratch_shapes=[
                pltpu.VMEM((height + 2 * ambit, tile), F32),
                pltpu.VMEM((tile, tile), F32),
                pltpu.VMEM((kernels, wide, wide), BF16),
                pltpu.VMEM((kernels, wide, wide), BF16),
                pltpu.VMEM((kernels, wide, wide), BF16),
                pltpu.VMEM((kernels, wide, wide), BF16),
                pltpu.VMEM((kernels, 2, tile, extent), BF16),
                pltpu.VMEM((kernels, 2 * tile, wide), F32),
                pltpu.VMEM((2 * tile, LANES), F32),
                pltpu.VMEM((3, kernels, wide, wide), BF16),
                pltpu.SemaphoreType.DMA((2,)),
            ],
            compiler_params=pltpu.CompilerParams(vmem_limit_bytes=48 * 1024 * 1024),
        )(mask, target_print, flags, taps, dose_factor, halos)

        def device(q, column):
            return q * tile_count + column

        def moved(block, shift, step):
            pairs = [
                (device(q, i), device((q + step) % pw_count, i + shift))
                for q in range(pw_count) for i in range(tile_count) if 0 <= i + shift < tile_count]
            return lax.ppermute(block, ("pw", "tile"), pairs)

        sent = [lax.rem(p + step, pw_count) for step in range(pw_count)]
        centers = [moved(center[sent[step]], 0, step) for step in range(1, pw_count)]
        lefts = [moved(rims[sent[step]], 1, step) for step in range(pw_count)]
        rights = [moved(rims[sent[step]], -1, step) for step in range(pw_count)]
        count = 1 + len(centers) + len(lefts) + len(rights)
        return pl.pallas_call(
            gather,
            out_shape=jax.ShapeDtypeStruct((tile_rows, own_rows, tile), F32),
            in_specs=[smem, smem] + [vmem] * count,
            out_specs=vmem,
        )(flags, p.reshape(1), center, *centers, *lefts, *rights)

    return jax.shard_map(
        on_device,
        mesh=mesh,
        in_specs=(
            P(None, None, "tile"),
            P(None, None, "tile"),
            P(None, "tile"),
            P("pw", None, None, None),
            P("pw"),
        ),
        out_specs=P(None, "pw", "tile"),
        check_vma=False,
    )
```

time: 153 us -> 47.5 us (0.31); the launches traced: 151 us -> 47.2 us
  local copies, waits for them, and re-layouts: 54.3 us -> 1.48 us
  matrix products: 28.1 us -> 0 us
  waiting for transfers between devices: 26 us -> 9.46 us
  Pallas kernels: 0 us -> 15.6 us
  between operations: 15.4 us -> 0.87 us
  other arithmetic: 15.1 us -> 1.51 us
  starting transfers between devices: 12 us -> 18.3 us
    dot_general x4 -> x0, matrix products: 28.1 us -> none  [the longest x1 7.66 us: tile_gradient(): jnp.einsum('kts,ksf->ktf', weighted, adj_cols, preferred_element_type=jnp...]
    another operation x2 -> x0, local copies, waits for them, and re-layouts: 26.5 us -> none  [skew_band(): repeated = jnp.tile(padded, (1,) * len(lead) + (TILE,))]
    reduce_scatter x1 -> x0, waiting for transfers between devices: 22 us -> none  [on_device(): return lax.psum_scatter(owned, 'pw', scatter_dimension=1, tiled=True)]
    pallas_call x0 -> x2, Pallas kernels: none -> 15.6 us  [the longest x1 13.6 us: on_device(): pl.pallas_call(gradient, out_shape=(jax.ShapeDtypeStruct((pw_count, pack_...]
    reshape x2 -> x0, local copies, waits for them, and re-layouts: 13.2 us -> none  [the longest x1 13 us: skew_band(): return repeated[..., :TILE * EXTENT].reshape(lead + (TILE, EXTENT))]
    slice x4 -> x1, local copies, waits for them, and re-layouts: 9.02 us -> 0.14 us  [on_device(): mask[:, tile - ambit:].astype(BF16)]
    squeeze x1 -> x0, other arithmetic: 6.56 us -> none  [build_tables(): col_imag = bands[:, 3]]
    ppermute x4 -> x7, starting transfers between devices: 12 us -> 18.3 us  [the longest x5 11.8 us: moved(): return lax.ppermute(block, ('pw', 'tile'), pairs)]
  transfers between devices with their start and end apart: 5 -> 7, of which waited for: 3 -> 4; matrix products, arithmetic and copies ran while one was open for 41% -> 0% of each run, Pallas kernels for 0% -> 0%
where the time goes in v1:
time: 47.5 us; the launch traced here: 47.2 us
  starting transfers between devices  18.3 us (39%)
  Pallas kernels  15.6 us (33%)
  waiting for transfers between devices  9.46 us (20%)
  other arithmetic  1.51 us (3%)
  local copies, waits for them, and re-layouts  1.48 us (3%)
  between operations  0.87 us (2%)
    pallas_call x1, Pallas kernels, on_device(): pl.pallas_call(gradient, out_shape=(jax.ShapeDtypeStruct((pw_count, pack_...  13.6 us
    ppermute x5, starting transfers between devices, moved(): return lax.ppermute(block, ('pw', 'tile'), pairs)  11.8 us
    ppermute x1, starting transfers between devices, on_device(): lax.ppermute(mask[:, tile - ambit:].astype(BF16), 'tile', right_way)  4.63 us
    ppermute x1, waiting for transfers between devices, on_device(): after = lax.ppermute(mask[:, :ambit].astype(BF16), 'tile', left_way)  4.4 us
    ppermute x5, waiting for transfers between devices, moved(): return lax.ppermute(block, ('pw', 'tile'), pairs)  4.39 us
    pallas_call x1, Pallas kernels, on_device(): pl.pallas_call(gather, out_shape=jax.ShapeDtypeStruct((tile_rows, own_row...  2 us
    ppermute x1, starting transfers between devices, on_device(): after = lax.ppermute(mask[:, :ambit].astype(BF16), 'tile', left_way)  1.92 us
    another operation x1, other arithmetic  1.37 us
  transfers between devices with their start and end apart: 7, of which 4 were waited for; matrix products, arithmetic and copies ran while one was open for 0% of the time, Pallas kernels for 0%

profile of v1, /device:TPU:1, one launch (start us, length us, event | category | flops | bytes accessed | tf_op | source)
XLA Modules:
  0.0 47.2 jit_solution(7753937443781314223)
XLA Ops:
  0.0 0.0 copy-start.1
  0.0 1.4 %bitcast_convert_fusion = bf16[1024,256]{1,0:T(8,128)(2,1)S(1)} fusion(f32[4,256,256]{2,1,0:T(8,128)} %param.5), kind=kLoop, calls=%fused_computation.9 | loop fusion | flops 262144 | bytes 1572864 | tf_op jit(solution)/shard_map/convert.1
  1.4 0.0 copy-start
  1.4 0.1 fusion.4
  1.5 0.0 copy-start.9
  1.5 4.6 %collective-permute-start = (bf16[1024,64]{1,0:T(8,128)(2,1)S(1)}, bf16[1024,64]{1,0:T(8,128)(2,1)S(1)}, u32[]{:S(2)}, u32[]{:S(2)}) collective-permute-start(bf16[1024,64]{1,0:T(8,128)(2,1)S(1)} %get-tuple-element.9), channel_id=1, source_target_pairs={{0,1},{1,2},{2,3},{3,4},{4,5},{5,6},{6,7},{7,8},{8,9},{9,10},{10,1... | collective-permute-start | bytes 393224 | tf_op jit(solution)/shard_map/ppermute | solution.py:219
  6.2 1.9 %collective-permute-start.1 = (bf16[1024,64]{1,0:T(8,128)(2,1)S(1)}, bf16[1024,64]{1,0:T(8,128)(2,1)S(1)}, u32[]{:S(2)}, u32[]{:S(2)}) collective-permute-start(bf16[1024,64]{1,0:T(8,128)(2,1)S(1)} %get-tuple-element.10), channel_id=1, source_target_pairs={{1,0},{2,1},{3,2},{4,3},{5,4},{6,5},{7,6},{8,7},{9,8},{10,9},{11,1... | collective-permute-start | bytes 393224 | tf_op jit(solution)/shard_map/ppermute | solution.py:220
  8.8 0.0 copy-done.9
  8.8 0.7 %collective-permute-done = bf16[1024,64]{1,0:T(8,128)(2,1)S(1)} collective-permute-done((bf16[1024,64]{1,0:T(8,128)(2,1)S(1)}, bf16[1024,64]{1,0:T(8,128)(2,1)S(1)}, u32[]{:S(2)}, u32[]{:S(2)}) %collective-permute-start) | collective-permute-done | bytes 131104 | tf_op jit(solution)/shard_map/ppermute | solution.py:219
  9.5 4.4 %collective-permute-done.1 = bf16[1024,64]{1,0:T(8,128)(2,1)S(1)} collective-permute-done((bf16[1024,64]{1,0:T(8,128)(2,1)S(1)}, bf16[1024,64]{1,0:T(8,128)(2,1)S(1)}, u32[]{:S(2)}, u32[]{:S(2)}) %collective-permute-start.1) | collective-permute-done | bytes 131104 | tf_op jit(solution)/shard_map/ppermute | solution.py:220
  13.9 0.1 fusion.3.refs_5_
  14.0 0.0 copy-start.3
  14.0 0.0 copy-done.1
  14.0 0.0 copy-done
  14.1 0.6 %copy-done.3 = s32[4,1]{0,1:T(1,128)S(1)} copy-done((s32[4,1]{0,1:T(1,128)S(1)}, s32[4,1]{0,1:T(1,128)}, u32[]{:S(2)}) %copy-start.3) | copy-done | bytes 40
  14.7 13.6 %shard_map.55 = (bf16[2,192,256]{2,1,0:T(8,128)(2,1)S(1)}, bf16[2,208,128]{2,1,0:T(8,128)(2,1)S(1)}) custom-call(f32[1024,256]{1,0:T(8,128)S(1)} %bitcast.11, f32[4,256,256]{2,1,0:T(8,128)S(1)} %copy-done.1, s32[4]{0:T(128)S(1)} %bitcast.13, f32[12,8,256]{2,1,0:T(8,128)S(1)} %pad.8.refs_3_, f32[1]{0:T(128)S(6)} %copy.6.refs_4_, ...), custom_call_target="tpu_custom_call" | custom-call | tf_op jit(solution)/shard_map/pallas_call | solution.py:229
  28.3 0.0 copy-start.2
  28.3 1.3 %collective-permute-start.2 = (bf16[192,256]{1,0:T(8,128)(2,1)S(1)}, bf16[192,256]{1,0:T(8,128)(2,1)S(1)}, u32[]{:S(2)}, u32[]{:S(2)}) collective-permute-start(bf16[192,256]{1,0:T(8,128)(2,1)S(1)} %dynamic-slice_bitcast_fusion), channel_id=1, source_target_pairs={{0,16},{1,17},{2,18},{3,19},{4,20},{5,21},{6,22},{7,23},{8,24},{9,... | collective-permute-start | bytes 294920 | tf_op jit(solution)/shard_map/ppermute | solution.py:260
  29.6 0.0 copy-done.2
  29.6 2.0 %collective-permute-start.3 = (bf16[208,128]{1,0:T(8,128)(2,1)S(1)}, bf16[208,128]{1,0:T(8,128)(2,1)S(1)}, u32[]{:S(2)}, u32[]{:S(2)}) collective-permute-start(bf16[208,128]{1,0:T(8,128)(2,1)S(1)} %get-tuple-element.12), channel_id=1, source_target_pairs={{0,1},{1,2},{2,3},{3,4},{4,5},{5,6},{6,7},{7,8},{8,9},{9,10},{10,1... | collective-permute-start | bytes 159752 | tf_op jit(solution)/shard_map/ppermute | solution.py:260
  31.7 4.6 %collective-permute-start.4 = (bf16[208,128]{1,0:T(8,128)(2,1)S(1)}, bf16[208,128]{1,0:T(8,128)(2,1)S(1)}, u32[]{:S(2)}, u32[]{:S(2)}) collective-permute-start(bf16[208,128]{1,0:T(8,128)(2,1)S(1)} %get-tuple-element.11), channel_id=1, source_target_pairs={{0,17},{1,18},{2,19},{3,20},{4,21},{5,22},{6,23},{7,24},{8,25},{9,... | collective-permute-start | bytes 159752 | tf_op jit(solution)/shard_map/ppermute | solution.py:260
  36.3 1.9 %collective-permute-start.5 = (bf16[208,128]{1,0:T(8,128)(2,1)S(1)}, bf16[208,128]{1,0:T(8,128)(2,1)S(1)}, u32[]{:S(2)}, u32[]{:S(2)}) collective-permute-start(bf16[208,128]{1,0:T(8,128)(2,1)S(1)} %get-tuple-element.12), channel_id=1, source_target_pairs={{1,0},{2,1},{3,2},{4,3},{5,4},{6,5},{7,6},{8,7},{9,8},{10,9},{11,1... | collective-permute-start | bytes 159752 | tf_op jit(solution)/shard_map/ppermute | solution.py:260
  38.2 1.9 %collective-permute-start.6 = (bf16[208,128]{1,0:T(8,128)(2,1)S(1)}, bf16[208,128]{1,0:T(8,128)(2,1)S(1)}, u32[]{:S(2)}, u32[]{:S(2)}) collective-permute-start(bf16[208,128]{1,0:T(8,128)(2,1)S(1)} %get-tuple-element.11), channel_id=1, source_target_pairs={{1,16},{2,17},{3,18},{4,19},{5,20},{6,21},{7,22},{8,23},{9,24},{10... | collective-permute-start | bytes 159752 | tf_op jit(solution)/shard_map/ppermute | solution.py:260
  40.1 0.0 collective-permute-done.3.refs_4_
  40.2 0.0 copy-start.5
  40.2 0.0 collective-permute-done.4.refs_5_
  40.2 0.0 copy-start.6
  40.2 1.6 %collective-permute-done.5.refs_6_ = bf16[208,128]{1,0:T(8,128)(2,1)S(1)} collective-permute-done((bf16[208,128]{1,0:T(8,128)(2,1)S(1)}, bf16[208,128]{1,0:T(8,128)(2,1)S(1)}, u32[]{:S(2)}, u32[]{:S(2)}) %collective-permute-start.5) | collective-permute-done | bytes 53280 | tf_op jit(solution)/shard_map/ppermute | solution.py:260
  41.7 0.0 copy-start.7
  41.7 2.8 %collective-permute-done.6.refs_7_ = bf16[208,128]{1,0:T(8,128)(2,1)S(1)} collective-permute-done((bf16[208,128]{1,0:T(8,128)(2,1)S(1)}, bf16[208,128]{1,0:T(8,128)(2,1)S(1)}, u32[]{:S(2)}, u32[]{:S(2)}) %collective-permute-start.6) | collective-permute-done | bytes 53280 | tf_op jit(solution)/shard_map/ppermute | solution.py:260
  44.6 0.0 copy-start.8
  44.6 0.0 collective-permute-done.2.refs_3_
  44.6 0.0 copy-start.4
  44.6 0.0 copy-done.5
  44.6 0.0 copy-done.6
  44.6 0.0 copy-done.7
  44.6 0.6 %copy-done.8 = bf16[208,128]{1,0:T(8,128)(2,1)} copy-done((bf16[208,128]{1,0:T(8,128)(2,1)}, bf16[208,128]{1,0:T(8,128)(2,1)S(1)}, u32[]{:S(2)}) %copy-start.8) | copy-done | bytes 53272
  45.2 0.1 copy-done.4
  45.2 2.0 %shard_map.56 = f32[4,128,256]{2,1,0:T(8,128)} custom-call(s32[4]{0:T(128)} %bitcast.12, s32[1]{0:T(128)} %bitcast.1.refs_1_, bf16[2,192,256]{2,1,0:T(8,128)(2,1)} %copy-done.2, bf16[192,256]{1,0:T(8,128)(2,1)} %copy-done.4, bf16[208,128]{1,0:T(8,128)(2,1)} %copy-done.5, bf16[208,128]{1,0:T(8,128)(2,1)} %copy-done.6, bf16[208,128]{1,0:T(8,128)(2,1)} %copy-done.7, ...), custom_call_target="tpu_custom_call" | custom-call | tf_op jit(solution)/shard_map/pallas_call | solution.py:267
  (3 shorter events, 0.0 us)
Async XLA Ops:
  0.0 14.0 %copy-start.1 = (f32[4,256,256]{2,1,0:T(8,128)S(1)}, f32[4,256,256]{2,1,0:T(8,128)}, u32[]{:S(2)}) copy-start(f32[4,256,256]{2,1,0:T(8,128)} %refs_1_.1) | copy-start | bytes 3145732
  1.4 12.7 %copy-start = (f32[4,256,256]{2,1,0:T(8,128)S(1)}, f32[4,256,256]{2,1,0:T(8,128)}, u32[]{:S(2)}) copy-start(f32[4,256,256]{2,1,0:T(8,128)} %param.5) | copy-start | bytes 3145732
  1.5 7.2 %copy-start.9 = (f32[1,12,4,129]{3,2,1,0:T(4,128)S(1)}, f32[1,12,4,129]{3,2,1,0:T(4,128)}, u32[]{:S(2)}) copy-start(f32[1,12,4,129]{3,2,1,0:T(4,128)} %param.8) | copy-start | bytes 74308
  1.5 7.9 %collective-permute-start = (bf16[1024,64]{1,0:T(8,128)(2,1)S(1)}, bf16[1024,64]{1,0:T(8,128)(2,1)S(1)}, u32[]{:S(2)}, u32[]{:S(2)}) collective-permute-start(bf16[1024,64]{1,0:T(8,128)(2,1)S(1)} %get-tuple-element.9), channel_id=1, source_target_pairs={{0,1},{1,2},{2,3},{3,4},{4,5},{5,6},{6,7},{7,8},{8,9},{9,10},{10,1... | collective-permute-start | bytes 393224 | tf_op jit(solution)/shard_map/ppermute | solution.py:219
  6.2 7.7 %collective-permute-start.1 = (bf16[1024,64]{1,0:T(8,128)(2,1)S(1)}, bf16[1024,64]{1,0:T(8,128)(2,1)S(1)}, u32[]{:S(2)}, u32[]{:S(2)}) collective-permute-start(bf16[1024,64]{1,0:T(8,128)(2,1)S(1)} %get-tuple-element.10), channel_id=1, source_target_pairs={{1,0},{2,1},{3,2},{4,3},{5,4},{6,5},{7,6},{8,7},{9,8},{10,9},{11,1... | collective-permute-start | bytes 393224 | tf_op jit(solution)/shard_map/ppermute | solution.py:220
  14.0 0.7 %copy-start.3 = (s32[4,1]{0,1:T(1,128)S(1)}, s32[4,1]{0,1:T(1,128)}, u32[]{:S(2)}) copy-start(s32[4,1]{0,1:T(1,128)} %param.7) | copy-start | bytes 52
  28.3 1.3 %copy-start.2 = (bf16[2,192,256]{2,1,0:T(8,128)(2,1)}, bf16[2,192,256]{2,1,0:T(8,128)(2,1)S(1)}, u32[]{:S(2)}) copy-start(bf16[2,192,256]{2,1,0:T(8,128)(2,1)S(1)} %get-tuple-element.7.refs_2_) | copy-start | bytes 589828
  28.3 16.3 %collective-permute-start.2 = (bf16[192,256]{1,0:T(8,128)(2,1)S(1)}, bf16[192,256]{1,0:T(8,128)(2,1)S(1)}, u32[]{:S(2)}, u32[]{:S(2)}) collective-permute-start(bf16[192,256]{1,0:T(8,128)(2,1)S(1)} %dynamic-slice_bitcast_fusion), channel_id=1, source_target_pairs={{0,16},{1,17},{2,18},{3,19},{4,20},{5,21},{6,22},{7,23},{8,24},{9,... | collective-permute-start | bytes 294920 | tf_op jit(solution)/shard_map/ppermute | solution.py:260
  29.6 10.5 %collective-permute-start.3 = (bf16[208,128]{1,0:T(8,128)(2,1)S(1)}, bf16[208,128]{1,0:T(8,128)(2,1)S(1)}, u32[]{:S(2)}, u32[]{:S(2)}) collective-permute-start(bf16[208,128]{1,0:T(8,128)(2,1)S(1)} %get-tuple-element.12), channel_id=1, source_target_pairs={{0,1},{1,2},{2,3},{3,4},{4,5},{5,6},{6,7},{7,8},{8,9},{9,10},{10,1... | collective-permute-start | bytes 159752 | tf_op jit(solution)/shard_map/ppermute | solution.py:260
  31.7 8.5 %collective-permute-start.4 = (bf16[208,128]{1,0:T(8,128)(2,1)S(1)}, bf16[208,128]{1,0:T(8,128)(2,1)S(1)}, u32[]{:S(2)}, u32[]{:S(2)}) collective-permute-start(bf16[208,128]{1,0:T(8,128)(2,1)S(1)} %get-tuple-element.11), channel_id=1, source_target_pairs={{0,17},{1,18},{2,19},{3,20},{4,21},{5,22},{6,23},{7,24},{8,25},{9,... | collective-permute-start | bytes 159752 | tf_op jit(solution)/shard_map/ppermute | solution.py:260
  36.3 5.5 %collective-permute-start.5 = (bf16[208,128]{1,0:T(8,128)(2,1)S(1)}, bf16[208,128]{1,0:T(8,128)(2,1)S(1)}, u32[]{:S(2)}, u32[]{:S(2)}) collective-permute-start(bf16[208,128]{1,0:T(8,128)(2,1)S(1)} %get-tuple-element.12), channel_id=1, source_target_pairs={{1,0},{2,1},{3,2},{4,3},{5,4},{6,5},{7,6},{8,7},{9,8},{10,9},{11,1... | collective-permute-start | bytes 159752 | tf_op jit(solution)/shard_map/ppermute | solution.py:260
  38.2 6.4 %collective-permute-start.6 = (bf16[208,128]{1,0:T(8,128)(2,1)S(1)}, bf16[208,128]{1,0:T(8,128)(2,1)S(1)}, u32[]{:S(2)}, u32[]{:S(2)}) collective-permute-start(bf16[208,128]{1,0:T(8,128)(2,1)S(1)} %get-tuple-element.11), channel_id=1, source_target_pairs={{1,16},{2,17},{3,18},{4,19},{5,20},{6,21},{7,22},{8,23},{9,24},{10... | collective-permute-start | bytes 159752 | tf_op jit(solution)/shard_map/ppermute | solution.py:260
  40.2 4.4 %copy-start.5 = (bf16[208,128]{1,0:T(8,128)(2,1)}, bf16[208,128]{1,0:T(8,128)(2,1)S(1)}, u32[]{:S(2)}) copy-start(bf16[208,128]{1,0:T(8,128)(2,1)S(1)} %collective-permute-done.3.refs_4_) | copy-start | bytes 159748
  40.2 4.4 %copy-start.6 = (bf16[208,128]{1,0:T(8,128)(2,1)}, bf16[208,128]{1,0:T(8,128)(2,1)S(1)}, u32[]{:S(2)}) copy-start(bf16[208,128]{1,0:T(8,128)(2,1)S(1)} %collective-permute-done.4.refs_5_) | copy-start | bytes 159748
  41.7 2.9 %copy-start.7 = (bf16[208,128]{1,0:T(8,128)(2,1)}, bf16[208,128]{1,0:T(8,128)(2,1)S(1)}, u32[]{:S(2)}) copy-start(bf16[208,128]{1,0:T(8,128)(2,1)S(1)} %collective-permute-done.5.refs_6_) | copy-start | bytes 159748
  44.6 0.6 %copy-start.8 = (bf16[208,128]{1,0:T(8,128)(2,1)}, bf16[208,128]{1,0:T(8,128)(2,1)S(1)}, u32[]{:S(2)}) copy-start(bf16[208,128]{1,0:T(8,128)(2,1)S(1)} %collective-permute-done.6.refs_7_) | copy-start | bytes 159748
  44.6 0.7 %copy-start.4 = (bf16[192,256]{1,0:T(8,128)(2,1)}, bf16[192,256]{1,0:T(8,128)(2,1)S(1)}, u32[]{:S(2)}) copy-start(bf16[192,256]{1,0:T(8,128)(2,1)S(1)} %collective-permute-done.2.refs_3_) | copy-start | bytes 294916

commit v2 on v1

--- a/solution.py
+++ b/solution.py
@@ -9,6 +9,7 @@
 THRESHOLD = 1.3
 LOSS_WEIGHT = 4.0
 LANES = 128
+MESH = pl.DeviceIdType.MESH
 F32 = jnp.float32
 BF16 = jnp.bfloat16
 
@@ -18,7 +19,7 @@
 
 
 def gradient_kernel(
-    sizes, mask_hbm, goal_hbm, flags, taps, dose, halos, center, rims,
+    sizes, mask_hbm, goal_hbm, flags, taps, dose, place, halos, center, rims,
     mask_f32, goal_f32, row_bands, row_bands_t, col_a, col_b,
     fields_in, fields, intensity, adjoint, local_sem,
 ):
@@ -141,6 +142,7 @@
         + [jnp.zeros((16 - tile_rows, LANES), F32)], axis=0)
     for q in range(pw_count):
         first = ambit + q * own_rows
+        slot = lax.rem(q - place[0] + pw_count, pw_count)
         if q * own_rows < ambit:
             edge = ambit + tile + q * own_rows
         else:
@@ -149,28 +151,102 @@
             main = block[first:first + own_rows].astype(BF16)
             side = block[edge:edge + edge_rows].astype(BF16)
             if b < 2:
-                center[q, 0:own_rows, b * LANES:(b + 1) * LANES] = main
-                center[q, own_rows:, b * LANES:(b + 1) * LANES] = side
+                center[slot, 0:own_rows, b * LANES:(b + 1) * LANES] = main
+                center[slot, own_rows:, b * LANES:(b + 1) * LANES] = side
             else:
-                rims[q, 0:own_rows, :] = main
-                rims[q, own_rows:pack_rows, :] = side
-                rims[q, pack_rows:, :] = flag_rows.astype(BF16)
-
-
-def gather_kernel(sizes, flags, place, own_center, *refs):
-    pw_count, tile_rows, tile, ambit = sizes
-    centers, lefts, rights = refs[:pw_count - 1], refs[pw_count - 1:2 * pw_count - 1], refs[2 * pw_count - 1:-1]
-    out_ref = refs[-1]
+                rims[slot, 0:own_rows, :] = main
+                rims[slot, own_rows:pack_rows, :] = side
+                rims[slot, pack_rows:, :] = flag_rows.astype(BF16)
+
+
+def greet(devices, has_left, has_right, pw_count, partners):
+    barrier = pltpu.get_barrier_semaphore()
+    p, c = lax.axis_index("pw"), lax.axis_index("tile")
+    for step in range(1, pw_count if partners else 1):
+        pl.semaphore_signal(barrier, inc=1, device_id=(lax.rem(p + step, pw_count), c), device_id_type=MESH)
+    for has, column in ((has_left, c - 1), (has_right, c + 1)):
+        @pl.when(has)
+        def _(column=column):
+            for q in devices:
+                pl.semaphore_signal(barrier, inc=1, device_id=(q, column), device_id_type=MESH)
+    neighbours = jnp.where(has_left, 1, 0) + jnp.where(has_right, 1, 0)
+    pl.semaphore_wait(barrier, neighbours * len(devices) + (pw_count - 1 if partners else 0))
+
+
+def halo_kernel(tile_count, to_right, to_left, from_left, from_right, send, recv):
+    p, c = lax.axis_index("pw"), lax.axis_index("tile")
+    has_left, has_right = c > 0, c < tile_count - 1
+    greet([p], has_left, has_right, 1, False)
+
+    def copy(side, column):
+        return pltpu.make_async_remote_copy(
+            src_ref=(to_right, to_left)[side], dst_ref=(from_left, from_right)[side],
+            send_sem=send.at[side], recv_sem=recv.at[side], device_id=(p, column), device_id_type=MESH)
+
+    for has, side, column in ((has_right, 0, c + 1), (has_left, 1, c - 1)):
+        @pl.when(has)
+        def _(side=side, column=column):
+            copy(side, column).start()
+    for has, side, column in ((has_right, 0, c + 1), (has_left, 1, c - 1)):
+        @pl.when(has)
+        def _(side=side, column=column):
+            copy(side, column).wait_send()
+            copy(1 - side, column).wait_recv()
+
+
+def exchange_kernel(
+    pw_count, tile_count, center, rims, centers, lefts, rights,
+    center_send, center_recv, rim_send_0, rim_recv_0, rim_send_1, rim_recv_1,
+):
+    p, c = lax.axis_index("pw"), lax.axis_index("tile")
+    has_left, has_right = c > 0, c < tile_count - 1
+    others = [lax.rem(p + step, pw_count) for step in range(pw_count)]
+    greet(others, has_left, has_right, pw_count, True)
+    rim_sems = ((rim_send_0, rim_recv_0), (rim_send_1, rim_recv_1))
+
+    def center_copy(step):
+        return pltpu.make_async_remote_copy(
+            src_ref=center.at[step], dst_ref=centers.at[step - 1], send_sem=center_send.at[step],
+            recv_sem=center_recv.at[step], device_id=(others[step], c), device_id_type=MESH)
+
+    def rim_copy(step, side, column):
+        return pltpu.make_async_remote_copy(
+            src_ref=rims.at[step], dst_ref=(lefts, rights)[side].at[step], send_sem=rim_sems[side][0].at[step],
+            recv_sem=rim_sems[side][1].at[step], device_id=(others[step], column), device_id_type=MESH)
+
+    for step in range(1, pw_count):
+        center_copy(step).start()
+    for has, side, column in ((has_right, 0, c + 1), (has_left, 1, c - 1)):
+        @pl.when(has)
+        def _(side=side, column=column):
+            for step in reversed(range(pw_count)):
+                rim_copy(step, side, column).start()
+    for step in range(1, pw_count):
+        center_copy(step).wait_send()
+        center_copy(step).wait_recv()
+    for has, side, column in ((has_right, 0, c + 1), (has_left, 1, c - 1)):
+        @pl.when(has)
+        def _(side=side, column=column):
+            for step in range(pw_count):
+                rim_copy(step, side, column).wait_send()
+                rim_copy(step, 1 - side, column).wait_recv()
+
+
+def gather_kernel(sizes, flags, place, own_center, centers, lefts, rights, out_ref):
+    pw_count, tile_count, tile_rows, tile, ambit = sizes
     own_rows = tile // pw_count
     edge_rows = min(own_rows, ambit)
     pack_rows = own_rows + edge_rows
     p = place[0]
-    total = own_center[p].astype(F32)
-    for ref in centers:
-        total += ref[...].astype(F32)
-    left, right = lefts[0][...].astype(F32), rights[0][...].astype(F32)
-    left_sum = sum(ref[0:pack_rows, :].astype(F32) for ref in lefts)
-    right_sum = sum(ref[0:pack_rows, :].astype(F32) for ref in rights)
+    c = place[1]
+    total = own_center[0].astype(F32)
+    for step in range(pw_count - 1):
+        total += centers[step].astype(F32)
+    left, right = lefts[0].astype(F32), rights[0].astype(F32)
+    left_sum = sum(lefts[step, 0:pack_rows, :].astype(F32) for step in range(pw_count))
+    right_sum = sum(rights[step, 0:pack_rows, :].astype(F32) for step in range(pw_count))
+    left, left_sum = (jnp.where(c > 0, value, 0.0) for value in (left, left_sum))
+    right, right_sum = (jnp.where(c < tile_count - 1, value, 0.0) for value in (right, right_sum))
     pack_low = low_lanes(pack_rows, ambit)
     left_sum = jnp.where(pack_low, left_sum, 0.0)
     right_sum = jnp.where(pack_low, 0.0, right_sum)
@@ -214,17 +290,37 @@
         taps = jnp.pad(kernel_taps[0], ((0, 0), (0, 8 - kinds), (0, wide - tap_count)))
         flags = geometry_flags.reshape(tile_rows)
         mask = mask_tiles.reshape(height, tile)
-        right_way = [(i, i + 1) for i in range(tile_count - 1)]
-        left_way = [(j, i) for i, j in right_way]
-        before = lax.ppermute(mask[:, tile - ambit:].astype(BF16), "tile", right_way)
-        after = lax.ppermute(mask[:, :ambit].astype(BF16), "tile", left_way)
-        halos = jnp.pad(jnp.concatenate([before, after], axis=1), ((ambit, ambit), (0, 0)))
+        c = lax.axis_index("tile")
+        place = jnp.stack([p, c]).astype(jnp.int32)
+        half = height // 2
+        rim_type = jax.ShapeDtypeStruct((half, LANES), BF16)
+
+        def packed(columns):
+            return jnp.concatenate([columns[:half], columns[half:]], axis=1).astype(BF16)
+
+        def unpacked(rim):
+            return jnp.concatenate([rim[:, :ambit], rim[:, ambit:]], axis=0)
+
+        def halo(*refs):
+            halo_kernel(tile_count, *refs)
+
+        before, after = pl.pallas_call(
+            halo,
+            out_shape=(rim_type, rim_type),
+            in_specs=[anywhere] * 2,
+            out_specs=(anywhere,) * 2,
+            scratch_shapes=[pltpu.SemaphoreType.DMA((2,))] * 2,
+            compiler_params=pltpu.CompilerParams(collective_id=1, has_side_effects=True),
+        )(packed(mask[:, tile - ambit:]), packed(mask[:, :ambit]))
+        before = jnp.where(c > 0, before, jnp.zeros_like(before))
+        after = jnp.where(c < tile_count - 1, after, jnp.zeros_like(after))
+        halos = jnp.pad(jnp.concatenate([unpacked(before), unpacked(after)], axis=1), ((ambit, ambit), (0, 0)))
 
         def gradient(*refs):
             gradient_kernel((pw_count, tile_rows, tile, kernels, ambit), *refs)
 
         def gather(*refs):
-            gather_kernel((pw_count, tile_rows, tile, ambit), *refs)
+            gather_kernel((pw_count, tile_count, tile_rows, tile, ambit), *refs)
 
         center, rims = pl.pallas_call(
             gradient,
@@ -232,7 +328,7 @@
                 jax.ShapeDtypeStruct((pw_count, pack_rows, tile), BF16),
                 jax.ShapeDtypeStruct((pw_count, pack_rows + 16, LANES), BF16),
             ),
-            in_specs=[anywhere, anywhere, smem, vmem, smem, vmem],
+            in_specs=[anywhere, anywhere, smem, vmem, smem, smem, vmem],
             out_specs=(vmem, vmem),
             scratch_shapes=[
                 pltpu.VMEM((height + 2 * ambit, tile), F32),
@@ -248,28 +344,29 @@
                 pltpu.SemaphoreType.DMA((2,)),
             ],
             compiler_params=pltpu.CompilerParams(vmem_limit_bytes=48 * 1024 * 1024),
-        )(mask, target_print, flags, taps, dose_factor, halos)
-
-        def device(q, column):
-            return q * tile_count + column
-
-        def moved(block, shift, step):
-            pairs = [
-                (device(q, i), device((q + step) % pw_count, i + shift))
-                for q in range(pw_count) for i in range(tile_count) if 0 <= i + shift < tile_count]
-            return lax.ppermute(block, ("pw", "tile"), pairs)
-
-        sent = [lax.rem(p + step, pw_count) for step in range(pw_count)]
-        centers = [moved(center[sent[step]], 0, step) for step in range(1, pw_count)]
-        lefts = [moved(rims[sent[step]], 1, step) for step in range(pw_count)]
-        rights = [moved(rims[sent[step]], -1, step) for step in range(pw_count)]
-        count = 1 + len(centers) + len(lefts) + len(rights)
+        )(mask, target_print, flags, taps, dose_factor, place, halos)
+
+        def exchange(*refs):
+            exchange_kernel(pw_count, tile_count, *refs)
+
+        centers, lefts, rights = pl.pallas_call(
+            exchange,
+            out_shape=(
+                jax.ShapeDtypeStruct((pw_count - 1, pack_rows, tile), BF16),
+                jax.ShapeDtypeStruct((pw_count, pack_rows + 16, LANES), BF16),
+                jax.ShapeDtypeStruct((pw_count, pack_rows + 16, LANES), BF16),
+            ),
+            in_specs=[anywhere] * 2,
+            out_specs=(anywhere,) * 3,
+            scratch_shapes=[pltpu.SemaphoreType.DMA((pw_count,))] * 6,
+            compiler_params=pltpu.CompilerParams(collective_id=2, has_side_effects=True),
+        )(center, rims)
         return pl.pallas_call(
             gather,
             out_shape=jax.ShapeDtypeStruct((tile_rows, own_rows, tile), F32),
-            in_specs=[smem, smem] + [vmem] * count,
+            in_specs=[smem, smem] + [vmem] * 4,
             out_specs=vmem,
-        )(flags, p.reshape(1), center, *centers, *lefts, *rights)
+        )(flags, place, center, centers, lefts, rights)
 
     return jax.shard_map(
         on_device,

time: 47.5 us -> 37.8 us (0.80)
  the two profiles are of different devices: /device:TPU:1 before, /device:TPU:23 now
where the time goes in v2:
time: 37.8 us; the launch traced here: 37.6 us
  Pallas kernels  30.5 us (81%)
  other arithmetic  3.32 us (9%)
  local copies, waits for them, and re-layouts  3.02 us (8%)
  between operations  0.8 us (2%)
    pallas_call x1, Pallas kernels, on_device(): pl.pallas_call(gradient, out_shape=(jax.ShapeDtypeStruct((pw_count, pack_...  13.6 us
    pallas_call x1, Pallas kernels, on_device(): pl.pallas_call(exchange, out_shape=(jax.ShapeDtypeStruct((pw_count - 1, p...  9.05 us
    pallas_call x1, Pallas kernels, on_device(): pl.pallas_call(halo, out_shape=(rim_type, rim_type), in_specs=[anywhere]...  5.75 us
    unnamed x16, local copies, waits for them, and re-layouts  2.65 us
    pallas_call x1, Pallas kernels, on_device(): pl.pallas_call(gather, out_shape=jax.ShapeDtypeStruct((tile_rows, own_row...  2.07 us
    another operation x1, other arithmetic  1.28 us
    select_n x1, other arithmetic, on_device(): before = jnp.where(c > 0, before, jnp.zeros_like(before))  0.96 us
    concatenate x1, other arithmetic, packed(): jnp.concatenate([columns[:half], columns[half:]], axis=1).astype(BF16)  0.85 us

profile of v2, /device:TPU:23, one launch (start us, length us, event | category | flops | bytes accessed | tf_op | source)
XLA Modules:
  0.0 37.6 jit_solution(13447029809288648213)
XLA Ops:
  0.0 1.3 %bitcast_convert_fusion = bf16[1024,256]{1,0:T(8,128)(2,1)S(1)} fusion(f32[4,256,256]{2,1,0:T(8,128)} %param.5), kind=kLoop, calls=%fused_computation.13 | loop fusion | flops 262144 | bytes 1572864 | tf_op jit(solution)/shard_map/convert.7
  1.3 0.1 fusion.5
  1.4 0.8 %pad_maximum_fusion = (bf16[512,128]{1,0:T(8,128)(2,1)}, bf16[512,128]{1,0:T(8,128)(2,1)}) fusion(bf16[512,64]{1,0:T(8,128)(2,1)S(1)} %get-tuple-element.21, bf16[512,64]{1,0:T(8,128)(2,1)S(1)} %get-tuple-element.22, bf16[512,64]{1,0:T(8,128)(2,1)S(1)} %get-tuple-element.20, bf16[512,64]{1,0:T(8,128)(2,1)S(1)} %get-tuple-element.19), kind=kLoop, calls=%fused_computation.8 | loop fusion | flops 524288 | bytes 524288 | tf_op jit(solution)/shard_map/concatenate | solution.py:299
  2.3 5.7 %shard_map.55 = (bf16[512,128]{1,0:T(8,128)(2,1)}, bf16[512,128]{1,0:T(8,128)(2,1)}) custom-call(bf16[512,128]{1,0:T(8,128)(2,1)} %get-tuple-element.27.refs_0_, bf16[512,128]{1,0:T(8,128)(2,1)} %get-tuple-element.28.refs_1_), custom_call_target="tpu_custom_call" | custom-call | tf_op jit(solution)/shard_map/pallas_call | solution.py:307
  8.0 0.0 copy-start.6
  8.0 1.0 %broadcast_select_fusion.1 = bf16[512,128]{1,0:T(8,128)(2,1)S(1)} fusion(bf16[512,128]{1,0:T(8,128)(2,1)} %get-tuple-element.12, pred[]{:T(512)S(6)} %gt.3), kind=kLoop, calls=%fused_computation.11 | loop fusion | flops 65536 | bytes 262145 | tf_op jit(solution)/shard_map/jit(_where)/select_n | solution.py:315
  9.0 0.0 copy-start
  9.0 0.0 copy-start.1
  9.0 0.1 fusion.6
  9.1 0.0 copy-done.6
  9.2 0.1 fusion.7
  9.3 0.0 copy-start.7
  9.3 0.2 fusion.1.refs_6_
  9.5 0.1 pad_add_fusion.refs_5_.refs_1_
  9.5 0.0 copy-start.5
  9.5 0.7 %copy-done.7 = f32[1,12,4,129]{3,2,1,0:T(4,128)S(1)} copy-done((f32[1,12,4,129]{3,2,1,0:T(4,128)S(1)}, f32[1,12,4,129]{3,2,1,0:T(4,128)}, u32[]{:S(2)}) %copy-start.7) | copy-done | bytes 24792
  10.9 0.0 copy-start.4
  10.9 0.0 copy-done.5
  10.9 0.0 copy-done
  10.9 0.0 copy-done.1
  10.9 0.6 %copy-done.4 = s32[4,1]{0,1:T(1,128)S(1)} copy-done((s32[4,1]{0,1:T(1,128)S(1)}, s32[4,1]{0,1:T(1,128)}, u32[]{:S(2)}) %copy-start.4) | copy-done | bytes 40
  11.6 13.6 %shard_map.56 = (bf16[2,192,256]{2,1,0:T(8,128)(2,1)S(1)}, bf16[2,208,128]{2,1,0:T(8,128)(2,1)S(1)}) custom-call(f32[1024,256]{1,0:T(8,128)S(1)} %bitcast.6, f32[4,256,256]{2,1,0:T(8,128)S(1)} %copy-done.1, s32[4]{0:T(128)S(1)} %bitcast.8, f32[12,8,256]{2,1,0:T(8,128)S(1)} %pad.8.refs_3_, f32[1]{0:T(128)S(6)} %copy.6.refs_4_, ...), custom_call_target="tpu_custom_call" | custom-call | tf_op jit(solution)/shard_map/pallas_call | solution.py:325
  25.2 0.0 copy-start.2
  25.2 0.7 %copy-done.2 = bf16[2,192,256]{2,1,0:T(8,128)(2,1)} copy-done((bf16[2,192,256]{2,1,0:T(8,128)(2,1)}, bf16[2,192,256]{2,1,0:T(8,128)(2,1)S(1)}, u32[]{:S(2)}) %copy-start.2) | copy-done | bytes 196632
  25.8 0.0 copy-start.3
  25.8 0.6 %copy-done.3 = bf16[2,208,128]{2,1,0:T(8,128)(2,1)} copy-done((bf16[2,208,128]{2,1,0:T(8,128)(2,1)}, bf16[2,208,128]{2,1,0:T(8,128)(2,1)S(1)}, u32[]{:S(2)}) %copy-start.3) | copy-done | bytes 106520
  26.5 9.1 %shard_map.57 = (bf16[1,192,256]{2,1,0:T(8,128)(2,1)}, bf16[2,208,128]{2,1,0:T(8,128)(2,1)}, bf16[2,208,128]{2,1,0:T(8,128)(2,1)}) custom-call(bf16[2,192,256]{2,1,0:T(8,128)(2,1)} %copy-done.2, bf16[2,208,128]{2,1,0:T(8,128)(2,1)} %copy-done.3), custom_call_target="tpu_custom_call" | custom-call | tf_op jit(solution)/shard_map/pallas_call | solution.py:352
  35.5 2.1 %shard_map.58 = f32[4,128,256]{2,1,0:T(8,128)} custom-call(s32[4]{0:T(128)} %bitcast.7, s32[2]{0:T(128)} %copy-done.5, bf16[2,192,256]{2,1,0:T(8,128)(2,1)} %copy-done.2, bf16[1,192,256]{2,1,0:T(8,128)(2,1)} %get-tuple-element.16.refs_3_, bf16[2,208,128]{2,1,0:T(8,128)(2,1)} %get-tuple-element.17.refs_4_, bf16[2,208,128]{2,1,0:T(8,128)(2,1)} %get-tuple-element.18.refs_5_), custom_call_target="tpu_custom_call" | custom-call | tf_op jit(solution)/shard_map/pallas_call | solution.py:364
  (2 shorter events, 0.0 us)
Async XLA Ops:
  8.0 1.1 %copy-start.6 = (bf16[512,128]{1,0:T(8,128)(2,1)S(1)}, bf16[512,128]{1,0:T(8,128)(2,1)}, u32[]{:S(2)}) copy-start(bf16[512,128]{1,0:T(8,128)(2,1)} %get-tuple-element.13) | copy-start | bytes 393220
  9.0 1.9 %copy-start = (f32[4,256,256]{2,1,0:T(8,128)S(1)}, f32[4,256,256]{2,1,0:T(8,128)}, u32[]{:S(2)}) copy-start(f32[4,256,256]{2,1,0:T(8,128)} %param.5) | copy-start | bytes 3145732
  9.0 1.9 %copy-start.1 = (f32[4,256,256]{2,1,0:T(8,128)S(1)}, f32[4,256,256]{2,1,0:T(8,128)}, u32[]{:S(2)}) copy-start(f32[4,256,256]{2,1,0:T(8,128)} %refs_1_.1) | copy-start | bytes 3145732
  9.3 0.9 %copy-start.7 = (f32[1,12,4,129]{3,2,1,0:T(4,128)S(1)}, f32[1,12,4,129]{3,2,1,0:T(4,128)}, u32[]{:S(2)}) copy-start(f32[1,12,4,129]{3,2,1,0:T(4,128)} %param.8) | copy-start | bytes 74308
  9.5 1.4 %copy-start.5 = (s32[2]{0:T(128)}, s32[2]{0:T(128)S(1)}, u32[]{:S(2)}) copy-start(s32[2]{0:T(128)S(1)} %pad_add_fusion.refs_5_.refs_1_) | copy-start | bytes 28
  10.9 0.7 %copy-start.4 = (s32[4,1]{0,1:T(1,128)S(1)}, s32[4,1]{0,1:T(1,128)}, u32[]{:S(2)}) copy-start(s32[4,1]{0,1:T(1,128)} %param.7) | copy-start | bytes 52
  25.2 0.7 %copy-start.2 = (bf16[2,192,256]{2,1,0:T(8,128)(2,1)}, bf16[2,192,256]{2,1,0:T(8,128)(2,1)S(1)}, u32[]{:S(2)}) copy-start(bf16[2,192,256]{2,1,0:T(8,128)(2,1)S(1)} %get-tuple-element.14.refs_0_.refs_2_) | copy-start | bytes 589828
  25.8 0.6 %copy-start.3 = (bf16[2,208,128]{2,1,0:T(8,128)(2,1)}, bf16[2,208,128]{2,1,0:T(8,128)(2,1)S(1)}, u32[]{:S(2)}) copy-start(bf16[2,208,128]{2,1,0:T(8,128)(2,1)S(1)} %get-tuple-element.15.refs_1_) | copy-start | bytes 319492
